TPU v7x, 32 devices: a whole 2x2x4 slice. The times are simulated.
32 devices in a mesh: grp: 2 (over y), occ: 4 (over z), aux: 4 (over x, core).
Axes of the slice: x: 2, y: 2, z: 4, core: 2. Of those that a mesh axis runs over, the one named last changes fastest.
Arguments:
- factors: float32 [8192, 3072], P(('grp', 'aux'), 'occ'), parts along dimension 0, may hold values from -0.75 to 0.75
- eps_occ: float32 [32], P('grp'), parts along dimension 0, may hold values from -2 to -0.5
- eps_vir: float32 [6144], P('grp'), parts along dimension 0, may hold values from 0.2 to 3
- tile_index: int32 [2], P('grp'), parts along dimension 0, may hold values from 0 to 15
- pair_offset: int32 [2], P('grp'), parts along dimension 0, may hold values from 1 to 3
Outputs:
- gradient: float32 [8192, 3072], P(('grp', 'aux'), 'occ'), parts along dimension 0
There are 2 independent parts, one for each index of `grp`. A program takes and returns all parts, laid end to end along the dimension named above; each array names one. Nothing has to cross between parts.
All inputs are finite; a program needn't handle non-finite values.
Results may differ from a plain program's by a relative error of at most 0.0001.
Values sent between devices are 32-bit elements; how exact they have to be, the bound alone decides.
A program may use at most 64 MiB of HBM per device.

v0:
```python
import jax
import jax.numpy as jnp
from jax import lax
from jax.sharding import PartitionSpec as P

VT = 192
BLK = 4
DMAX = 3


PRECISE = lax.Precision.HIGHEST


def shifted(x, axis, by):
    count = lax.axis_size(axis)
    return lax.ppermute(x, axis, [(i, (i + by) % count) for i in range(count)])


def inner_dot(left, right):
    return lax.dot_general(
        left, right, (((0,), (0,)), ((), ())), precision=PRECISE, preferred_element_type=jnp.float32
    )


def fetch_partner(factors, offset):
    holding = factors
    for bit_index in range(DMAX.bit_length()):
        arrived = shifted(holding, "occ", 1 << bit_index)
        holding = jnp.where(offset >> bit_index & 1 == 1, arrived, holding)
    return holding


def return_terms(far_grad, offset):
    holding = far_grad
    for bit_index in range(DMAX.bit_length()):
        arrived = shifted(holding, "occ", -(1 << bit_index))
        holding = jnp.where(offset >> bit_index & 1 == 1, arrived, holding)
    return holding


def local(factors, eps_occ, eps_vir, tile_index, pair_offset):
    tile_width = factors.shape[1]
    block_count = lax.axis_size("occ")
    my_block = lax.axis_index("occ")
    aux_count = lax.axis_size("aux")
    aux_rank = lax.axis_index("aux")
    share_rows = tile_width // aux_count
    vir_energy = lax.dynamic_slice_in_dim(eps_vir, tile_index[0] * VT, VT)
    block_energy = eps_occ.reshape(block_count, BLK)
    own_gaps = (vir_energy[None, :] - block_energy[my_block][:, None]).reshape(tile_width)
    offset = pair_offset[0]
    partner = fetch_partner(factors, offset)
    other_block = (my_block - offset) % block_count
    far_gaps = (vir_energy[None, :] - block_energy[other_block][:, None]).reshape(tile_width)
    columns = factors
    pair_ints = lax.psum_scatter(
        inner_dot(columns, partner), "aux", scatter_dimension=0, tiled=True
    )
    row_gaps = lax.dynamic_slice_in_dim(own_gaps, aux_rank * share_rows, share_rows)
    amplitude = pair_ints / (row_gaps[:, None] + far_gaps[None, :])
    shard_rows = lax.all_gather(amplitude, "aux", axis=0, tiled=True)
    product = jnp.dot(partner, shard_rows.T, precision=PRECISE, preferred_element_type=jnp.float32)
    columns = factors
    far_total = jnp.dot(columns, shard_rows, precision=PRECISE, preferred_element_type=jnp.float32)
    gradient = product + return_terms(far_total, offset)
    return gradient


def solution(mesh):
    in_specs = (P(("grp", "aux"), "occ"), P("grp"), P("grp"), P("grp"), P("grp"))
    out_specs = P(("grp", "aux"), "occ")
    return jax.shard_map(local, mesh=mesh, in_specs=in_specs, out_specs=out_specs, check_vma=False)
```

profile of v0, /device:TPU:0, one launch (start us, length us, event | category | flops | bytes accessed | tf_op | source)
XLA Modules:
  0.0 528.7 jit_solution(18040777457274245982)
XLA Ops:
  6.5 0.0 reduce-scatter.4.cloned.1.call-start
  6.5 3.1 collective-permute-start
  10.2 69.8 %collective-permute-done = f32[1024,768]{1,0:T(8,128)} collective-permute-done((f32[1024,768]{1,0:T(8,128)}, f32[1024,768]{1,0:T(8,128)}, u32[]{:S(2)}, u32[]{:S(2)}) %collective-permute-start) | collective-permute-done | bytes 3145760 | tf_op jit(solution)/shard_map/ppermute | solution.py:16
  80.0 2.3 broadcast_select_fusion.1
  82.3 0.8 collective-permute-start.1
  83.1 135.8 %collective-permute-done.1 = f32[1024,768]{1,0:T(8,128)} collective-permute-done((f32[1024,768]{1,0:T(8,128)S(1)}, f32[1024,768]{1,0:T(8,128)}, u32[]{:S(2)}, u32[]{:S(2)}) %collective-permute-start.1) | collective-permute-done | bytes 3145760 | tf_op jit(solution)/shard_map/ppermute | solution.py:16
  218.9 11.1 %convolution_bitcast_fusion.1 = f32[768,768]{0,1:T(8,128)} fusion(f32[1024,768]{1,0:T(8,128)} %param.5, f32[1024,768]{1,0:T(8,128)} %collective-permute-done.1, f32[1024,768]{1,0:T(8,128)S(1)} %broadcast_select_fusion.1, pred[]{:T(512)S(6)} %eq.10), kind=kOutput, calls=%fused_computation.2 | convolution fusion | flops 7248543744 | bytes 11796481 | tf_op jit(solution)/shard_map/dot_general | solution.py:20
  230.0 0.0 copy-start.1
  230.0 3.1 copy.12
  233.2 0.0 reduce-scatter.4.cloned.1.call-update
  233.2 0.2 all-gather.2.cloned.1.call-start
  234.1 0.0 copy-done.1
  234.1 0.1 reshape.27
  234.2 0.8 dynamic_slice.12
  235.0 0.1 broadcast_subtract_fusion.1
  235.0 0.1 sub.46
  235.1 0.1 sub.51
  235.2 0.1 dynamic_slice.14
  235.3 31.0 %reduce-scatter.4.cloned.1.call-done = f32[192,768]{1,0:T(8,128)} async-done(((f32[768,768]{1,0:T(8,128)}), f32[192,768]{1,0:T(8,128)}) %reduce-scatter.4.cloned.1.call-update) | async-done | bytes 589840 | tf_op jit(solution)/shard_map/reduce_scatter | solution.py:56
  266.3 2.0 add_divide_fusion
  268.3 0.0 all-gather.2.cloned.1.call-update
  268.3 24.2 %all-gather.2.cloned.1.call-done = f32[768,768]{1,0:T(8,128)} async-done(((f32[192,768]{1,0:T(8,128)}), f32[768,768]{1,0:T(8,128)}) %all-gather.2.cloned.1.call-update) | async-done | bytes 2359312 | tf_op jit(solution)/shard_map/all_gather | solution.py:61
  292.5 10.3 %convolution_bitcast_fusion = f32[1024,768]{1,0:T(8,128)S(1)} fusion(f32[768,768]{1,0:T(8,128)} %all-gather.2.cloned.1.call-done, f32[1024,768]{1,0:T(8,128)} %param.5), kind=kOutput, calls=%fused_computation.1 | convolution fusion | flops 7247757312 | bytes 8650752 | tf_op jit(solution)/shard_map/dot_general | solution.py:64
  302.8 0.0 copy-start
  302.8 3.6 collective-permute-start.2
  306.4 67.8 %collective-permute-done.2 = f32[1024,768]{1,0:T(8,128)S(1)} collective-permute-done((f32[1024,768]{1,0:T(8,128)S(1)}, f32[1024,768]{1,0:T(8,128)S(1)}, u32[]{:S(2)}, u32[]{:S(2)}) %collective-permute-start.2) | collective-permute-done | bytes 3145760 | tf_op jit(solution)/shard_map/ppermute | solution.py:16
  374.2 0.4 broadcast_select_fusion
  374.6 1.6 collective-permute-start.3
  376.2 136.1 %collective-permute-done.3 = f32[1024,768]{1,0:T(8,128)S(1)} collective-permute-done((f32[1024,768]{1,0:T(8,128)S(1)}, f32[1024,768]{1,0:T(8,128)S(1)}, u32[]{:S(2)}, u32[]{:S(2)}) %collective-permute-start.3) | collective-permute-done | bytes 3145760 | tf_op jit(solution)/shard_map/ppermute | solution.py:16
  512.4 0.0 copy-done
  512.4 9.5 %select_add_fusion = f32[1024,768]{1,0:T(8,128)} fusion(f32[1024,768]{1,0:T(8,128)S(1)} %collective-permute-done.3, f32[1024,768]{1,0:T(8,128)S(1)} %broadcast_select_fusion, f32[768,768]{1,0:T(8,128)S(1)} %copy-done, pred[]{:T(512)S(6)} %eq.10, f32[1024,768]{1,0:T(8,128)} %collective-permute-done.1, f32[1024,768]{1,0:T(8,128)S(1)} %broadcast_select_fusion.1), kind=kOutput, calls=%fused_computation | convolution fusion | flops 7250116608 | bytes 18087936 | tf_op jit(solution)/shard_map/dot_general | solution.py:62
  (1 shorter events, 0.0 us)
Async XLA Ops:
  6.5 259.7 %reduce-scatter.4.cloned.1.call-start = ((), (), s32[]{:S(2)}) async-start(), calls=%async_computation.2 | async-start | bytes 2949120 | tf_op jit(solution)/shard_map/reduce_scatter | solution.py:56
  6.5 73.5 %collective-permute-start = (f32[1024,768]{1,0:T(8,128)}, f32[1024,768]{1,0:T(8,128)}, u32[]{:S(2)}, u32[]{:S(2)}) collective-permute-start(f32[1024,768]{1,0:T(8,128)} %param.5), channel_id=1, source_target_pairs={{0,4},{4,8},{8,12},{12,0},{1,5},{5,9},{9,13},{13,1},{2,6},{6,10},{... | collective-permute-start | bytes 9437192 | tf_op jit(solution)/shard_map/ppermute | solution.py:16
  82.3 136.6 %collective-permute-start.1 = (f32[1024,768]{1,0:T(8,128)S(1)}, f32[1024,768]{1,0:T(8,128)}, u32[]{:S(2)}, u32[]{:S(2)}) collective-permute-start(f32[1024,768]{1,0:T(8,128)S(1)} %broadcast_select_fusion.1), channel_id=1, source_target_pairs={{0,8},{4,12},{8,0},{12,4},{1,9},{5,13},{9,1},{13,5},{2,10},{6,14},... | collective-permute-start | bytes 9437192 | tf_op jit(solution)/shard_map/ppermute | solution.py:16
  230.0 4.1 copy-start.1
  233.2 59.3 %all-gather.2.cloned.1.call-start = ((), (), s32[]{:S(2)}) async-start(), calls=%async_computation.1 | async-start | bytes 2949120 | tf_op jit(solution)/shard_map/all_gather | solution.py:61
  302.8 209.5 %copy-start = (f32[768,768]{1,0:T(8,128)S(1)}, f32[768,768]{1,0:T(8,128)}, u32[]{:S(2)}) copy-start(f32[768,768]{1,0:T(8,128)} %all-gather.2.cloned.1.call-done) | copy-start | bytes 7077892
  302.8 71.4 %collective-permute-start.2 = (f32[1024,768]{1,0:T(8,128)S(1)}, f32[1024,768]{1,0:T(8,128)S(1)}, u32[]{:S(2)}, u32[]{:S(2)}) collective-permute-start(f32[1024,768]{1,0:T(8,128)S(1)} %convolution_bitcast_fusion), channel_id=1, source_target_pairs={{0,12},{4,0},{8,4},{12,8},{1,13},{5,1},{9,5},{13,9},{2,14},{6,2},{... | collective-permute-start | bytes 9437192 | tf_op jit(solution)/shard_map/ppermute | solution.py:16
  374.6 137.8 %collective-permute-start.3 = (f32[1024,768]{1,0:T(8,128)S(1)}, f32[1024,768]{1,0:T(8,128)S(1)}, u32[]{:S(2)}, u32[]{:S(2)}) collective-permute-start(f32[1024,768]{1,0:T(8,128)S(1)} %broadcast_select_fusion), channel_id=1, source_target_pairs={{0,8},{4,12},{8,0},{12,4},{1,9},{5,13},{9,1},{13,5},{2,10},{6,14},... | collective-permute-start | bytes 9437192 | tf_op jit(solution)/shard_map/ppermute | solution.py:16
Sparse Core Ops, SparseCore 0:
  233.3 32.9 reduce-scatter.3
  268.5 24.0 all-gather.1
where the time goes:
time: 530 us; the launch traced here: 529 us
  waiting for transfers between devices  465 us (88%)
  matrix products  30.9 us (6%)
  between operations  14.8 us (3%)
  starting transfers between devices  9.3 us (2%)
    ppermute x4, waiting for transfers between devices, shifted(): return lax.ppermute(x, axis, [(i, (i + by) % count) for i in range(count)])  410 us
    reduce_scatter x1, waiting for transfers between devices, local(): lax.psum_scatter(inner_dot(columns, partner), 'aux', scatter_dimension=0,...  31 us
    all_gather x1, waiting for transfers between devices, local(): shard_rows = lax.all_gather(amplitude, 'aux', axis=0, tiled=True)  24.2 us
    dot_general x1, matrix products, inner_dot(): lax.dot_general(left, right, (((0,), (0,)), ((), ())), precision=PRECISE,...  11.1 us
  transfers between devices with their start and end apart: 6, of which 6 were waited for; matrix products, arithmetic and copies ran while one was open for 0% of the time, Pallas kernels for 0%

commit v1 on v0

v1 whole, which is shorter than its diff:
```python
import jax
import jax.numpy as jnp
from jax import lax
from jax.sharding import PartitionSpec as P

VT = 192
BLK = 4
DMAX = 3
CHUNKS = 4
LINE = 4

PRECISE = lax.Precision.HIGH


def inner_dot(left, right):
    return lax.dot_general(
        left, right, (((0,), (0,)), ((), ())), precision=PRECISE, preferred_element_type=jnp.float32
    )


def outer_dot(left, right):
    return lax.dot_general(
        left, right, (((1,), (1,)), ((), ())), precision=PRECISE, preferred_element_type=jnp.float32
    )


def gaps_of(vir_energy, energies):
    return (vir_energy[None, :] - energies[:, None]).reshape(-1)


def amplitude_of(own, far, own_gaps, far_gaps, weight):
    aux_count = lax.axis_size("aux")
    aux_rank = lax.axis_index("aux")
    share = far.shape[1] // aux_count
    ints = lax.psum_scatter(inner_dot(far, own), "aux", scatter_dimension=0, tiled=True)
    gaps = lax.dynamic_slice_in_dim(far_gaps, aux_rank * share, share)
    amplitude = jnp.where(weight > 0, weight * (ints / (gaps[:, None] + own_gaps[None, :])), 0.0)
    return lax.all_gather(amplitude, "aux", axis=0, tiled=True)


def term(far, amplitude):
    return jnp.dot(far, amplitude, precision=PRECISE, preferred_element_type=jnp.float32)


def local_ring(factors, eps_occ, eps_vir, tile_index, pair_offset):
    count = lax.axis_size("occ")
    me = lax.axis_index("occ")
    vir_energy = lax.dynamic_slice_in_dim(eps_vir, tile_index[0] * VT, VT)
    energy = eps_occ.reshape(count, BLK)
    own_gaps = gaps_of(vir_energy, energy[me])
    offset = pair_offset[0]
    total = jnp.zeros_like(factors)
    for sign in (1, -1):
        far = factors
        held = factors
        for hop in range(1, DMAX + 1):
            held = lax.ppermute(held, "occ", [(i, (i + sign) % count) for i in range(count)])
            far = jnp.where(offset == hop, held, far)
        far_gaps = gaps_of(vir_energy, energy[(me - sign * offset) % count])
        total = total + term(far, amplitude_of(factors, far, own_gaps, far_gaps, jnp.float32(1)))
    return total


def local_line(factors, eps_occ, eps_vir, tile_index, pair_offset):
    count = lax.axis_size("occ")
    me = lax.axis_index("occ")
    vir_energy = lax.dynamic_slice_in_dim(eps_vir, tile_index[0] * VT, VT)
    energy = eps_occ.reshape(count, BLK)
    own_gaps = gaps_of(vir_energy, energy[me])
    odd = pair_offset[0] % 2 == 1
    inner = (me == 1) | (me == 2)
    lower = lax.ppermute(factors, "occ", [(i, i + 1) for i in range(count - 1)])
    upper = lax.ppermute(factors, "occ", [(i + 1, i) for i in range(count - 1)])
    near = jnp.where(me % 2 == 0, upper, lower)
    other = jnp.where(me % 2 == 0, lower, upper)
    near_block = jnp.where(me % 2 == 0, me + 1, me - 1)
    near_gaps = gaps_of(vir_energy, energy[near_block])
    near_amp = amplitude_of(factors, near, own_gaps, near_gaps, jnp.where(odd, 1.0, 0.0))
    total = term(near, near_amp)
    far_block = jnp.where(odd, jnp.where(me % 2 == 0, me - 1, me + 1), me + 2) % count
    far_gaps = gaps_of(vir_energy, energy[far_block])
    weight = jnp.where(odd, 1.0, 2.0)
    width = factors.shape[1] // CHUNKS
    for chunk in range(CHUNKS):
        cols = slice(chunk * width, (chunk + 1) * width)
        across = lax.ppermute(near[:, cols], "occ", [(1, 2), (2, 1)])
        relay = jnp.where(odd, across, other[:, cols])
        ends = lax.ppermute(relay, "occ", [(2, 3), (1, 0)])
        far = jnp.where(inner, jnp.where(odd, other[:, cols], across), ends)
        amp = amplitude_of(factors, far, own_gaps, far_gaps[cols], weight)
        total = total + term(far, amp)
    return total


def solution(mesh):
    in_specs = (P(("grp", "aux"), "occ"), P("grp"), P("grp"), P("grp"), P("grp"))
    out_specs = P(("grp", "aux"), "occ")
    body = local_line if mesh.shape["occ"] == LINE else local_ring
    return jax.shard_map(body, mesh=mesh, in_specs=in_specs, out_specs=out_specs, check_vma=False)
```

time: 530 us -> 378 us (0.71)
  waiting for transfers between devices: 465 us -> 234 us
  blocking collectives: 0 us -> 37.4 us
  other arithmetic: 4.8 us -> 20.9 us
  starting transfers between devices: 9.3 us -> 20.3 us
  matrix products: 30.9 us -> 38 us
  local copies, waits for them, and re-layouts: 4.23 us -> 11 us
    ppermute x4 -> x10, waiting for transfers between devices: 410 us -> 174 us  [the longest x4 108 us: local_line(): ends = lax.ppermute(relay, 'occ', [(2, 3), (1, 0)])]
    all_gather x0 -> x4, blocking collectives: none -> 37.4 us  [amplitude_of(): return lax.all_gather(amplitude, 'aux', axis=0, tiled=True)]
    reduce_scatter x1 -> x5, waiting for transfers between devices: 31 us -> 60.1 us  [amplitude_of(): lax.psum_scatter(inner_dot(far, own), 'aux', scatter_dimension=0, tiled=T...]
    all_gather x1, waiting for transfers between devices: 24.2 us -> 0.01 us  [amplitude_of(): return lax.all_gather(amplitude, 'aux', axis=0, tiled=True)]
    select_n x2 -> x6, other arithmetic: 2.69 us -> 20.8 us  [the longest x2 9.35 us: local_line(): far = jnp.where(inner, jnp.where(odd, other[:, cols], across), ends)]
    ppermute x4 -> x10, starting transfers between devices: 9.07 us -> 19.9 us  [the longest x1 7.23 us: local_line(): lower = lax.ppermute(factors, 'occ', [(i, i + 1) for i in range(count - 1)])]
    dot_general x1 -> x5, matrix products: 11.1 us -> 16.2 us  [inner_dot(): lax.dot_general(left, right, (((0,), (0,)), ((), ())), precision=PRECISE,...]
    dot_general x2 -> x5, matrix products: 19.8 us -> 21.8 us  [term(): jnp.dot(far, amplitude, precision=PRECISE, preferred_element_type=jnp.flo...]
  transfers between devices with their start and end apart: 6 -> 16, of which waited for: 6 -> 9; matrix products, arithmetic and copies ran while one was open for 0% -> 11% of each run, Pallas kernels for 0% -> 0%
where the time goes in v1:
time: 378 us; the launch traced here: 377 us
  waiting for transfers between devices  234 us (62%)
  matrix products  38 us (10%)
  blocking collectives  37.4 us (10%)
  other arithmetic  20.9 us (6%)
  starting transfers between devices  20.3 us (5%)
  between operations  15.1 us (4%)
  local copies, waits for them, and re-layouts  11 us (3%)
    ppermute x4, waiting for transfers between devices, local_line(): ends = lax.ppermute(relay, 'occ', [(2, 3), (1, 0)])  108 us
    ppermute x1, waiting for transfers between devices, local_line(): upper = lax.ppermute(factors, 'occ', [(i + 1, i) for i in range(count - 1)])  64.8 us
    reduce_scatter x5, waiting for transfers between devices, amplitude_of(): lax.psum_scatter(inner_dot(far, own), 'aux', scatter_dimension=0, tiled=T...  60.1 us
    all_gather x4, blocking collectives, amplitude_of(): return lax.all_gather(amplitude, 'aux', axis=0, tiled=True)  37.4 us
    dot_general x5, matrix products, term(): jnp.dot(far, amplitude, precision=PRECISE, preferred_element_type=jnp.flo...  21.8 us
    dot_general x5, matrix products, inner_dot(): lax.dot_general(left, right, (((0,), (0,)), ((), ())), precision=PRECISE,...  16.2 us
    select_n x2, other arithmetic, local_line(): far = jnp.where(inner, jnp.where(odd, other[:, cols], across), ends)  9.35 us
  transfers between devices with their start and end apart: 16, of which 9 were waited for; matrix products, arithmetic and copies ran while one was open for 11% of the time, Pallas kernels for 0%

profile of v1, /device:TPU:0, one launch (start us, length us, event | category | flops | bytes accessed | tf_op | source)
XLA Modules:
  0.0 377.1 jit_solution(6960506319142112641)
XLA Ops:
  6.5 3.5 copy.6
  10.1 1.3 collective-permute-start
  11.4 7.2 %collective-permute-start.1 = (f32[1024,768]{0,1:T(8,128)}, f32[1024,768]{0,1:T(8,128)}, u32[]{:S(2)}, u32[]{:S(2)}) collective-permute-start(f32[1024,768]{0,1:T(8,128)} %copy.6), channel_id=1, source_target_pairs={{0,4},{4,8},{8,12},{1,5},{5,9},{9,13},{2,6},{6,10},{10,14},{3,7},{... | collective-permute-start | bytes 9437192 | tf_op jit(solution)/shard_map/ppermute | solution.py:72
  18.6 64.8 %collective-permute-done = f32[1024,768]{0,1:T(8,128)} collective-permute-done((f32[1024,768]{0,1:T(8,128)}, f32[1024,768]{0,1:T(8,128)}, u32[]{:S(2)}, u32[]{:S(2)}) %collective-permute-start) | collective-permute-done | bytes 3145760 | tf_op jit(solution)/shard_map/ppermute | solution.py:73
  83.4 1.2 collective-permute-done.1
  84.6 5.5 %broadcast_select_fusion = (f32[1024,768]{0,1:T(8,128)}, f32[1024,768]{0,1:T(8,128)S(1)}) fusion(f32[1024,768]{0,1:T(8,128)} %collective-permute-done.1, f32[1024,768]{0,1:T(8,128)} %collective-permute-done, pred[]{:T(512)S(6)} %eq.22), kind=kLoop, calls=%fused_computation.1 | loop fusion | flops 1572864 | bytes 12582913 | tf_op jit(solution)/shard_map/jit(_where)/select_n | solution.py:75
  90.2 1.6 copy-done.1
  91.8 5.4 %fusion.9 = f32[768,768]{1,0:T(8,128)} fusion(f32[1024,768]{0,1:T(8,128)S(1)} %get-tuple-element.6, f32[1024,768]{1,0:T(8,128)S(1)} %copy-done), kind=kOutput, calls=%fused_computation.35 | convolution fusion | flops 3623878656 | bytes 8650752 | tf_op jit(solution)/shard_map/dot_general | solution.py:16
  97.2 0.0 reduce-scatter.6.cloned.1.call-update
  97.2 0.0 reduce-scatter.8.cloned.1.call-start
  97.3 3.6 fusion.7
  100.9 1.6 collective-permute-start.2
  103.1 1.6 collective-permute-start.4
  104.7 1.6 collective-permute-start.6
  106.3 1.6 collective-permute-start.8
  107.9 0.0 collective-permute-done.2
  107.9 2.6 slice_select_fusion.3
  110.5 1.3 collective-permute-start.3
  111.8 0.0 collective-permute-done.4
  111.8 32.5 %collective-permute-done.3 = f32[1024,192]{0,1:T(8,128)} collective-permute-done((f32[1024,192]{0,1:T(8,128)}, f32[1024,192]{0,1:T(8,128)}, u32[]{:S(2)}, u32[]{:S(2)}) %collective-permute-start.3) | collective-permute-done | bytes 786464 | tf_op jit(solution)/shard_map/ppermute | solution.py:88
  144.3 4.8 %select_select_fusion.3 = (f32[1024,192]{0,1:T(8,128)S(1)}, f32[1024,192]{0,1:T(8,128)}, f32[1024,192]{0,1:T(8,128)}, f32[1024,192]{0,1:T(8,128)}) fusion(f32[1024,192]{0,1:T(8,128)} %collective-permute-done.3, f32[1024,192]{0,1:T(8,128)} %collective-permute-done.2, f32[1024,768]{0,1:T(8,128)} %get-tuple-element.5, pred[]{:T(512)S(6)} %eq.23, pred[]{:T(512)S(6)} %or.3, ...), kind=kLoop, calls=%fused_computation.6 | loop fusion | flops 983040 | bytes 10223618 | tf_op jit(solution)/shard_map/jit(_where)/select_n | solution.py:89
  149.1 1.3 collective-permute-start.5
  150.4 1.3 collective-permute-start.7
  151.7 1.3 collective-permute-start.9
  153.0 2.1 fusion.11
  155.1 0.0 reduce-scatter.8.cloned.1.call-update
  155.1 0.0 reduce-scatter.10.cloned.1.call-start
  155.2 44.4 %collective-permute-done.5 = f32[1024,192]{0,1:T(8,128)} collective-permute-done((f32[1024,192]{0,1:T(8,128)}, f32[1024,192]{0,1:T(8,128)}, u32[]{:S(2)}, u32[]{:S(2)}) %collective-permute-start.5) | collective-permute-done | bytes 786464 | tf_op jit(solution)/shard_map/ppermute | solution.py:88
  199.6 16.9 %collective-permute-done.7 = f32[1024,192]{0,1:T(8,128)} collective-permute-done((f32[1024,192]{0,1:T(8,128)}, f32[1024,192]{0,1:T(8,128)}, u32[]{:S(2)}, u32[]{:S(2)}) %collective-permute-start.7) | collective-permute-done | bytes 786464 | tf_op jit(solution)/shard_map/ppermute | solution.py:88
  216.5 14.3 %collective-permute-done.9 = f32[1024,192]{0,1:T(8,128)} collective-permute-done((f32[1024,192]{0,1:T(8,128)}, f32[1024,192]{0,1:T(8,128)}, u32[]{:S(2)}, u32[]{:S(2)}) %collective-permute-start.9) | collective-permute-done | bytes 786464 | tf_op jit(solution)/shard_map/ppermute | solution.py:88
  230.8 4.6 %select_select_fusion.2 = (f32[1024,192]{0,1:T(8,128)S(1)}, f32[1024,192]{0,1:T(8,128)}, f32[1024,192]{0,1:T(8,128)}) fusion(f32[1024,192]{0,1:T(8,128)} %collective-permute-done.5, f32[1024,192]{0,1:T(8,128)} %collective-permute-done.4, f32[1024,768]{0,1:T(8,128)} %get-tuple-element.5, pred[]{:T(512)S(6)} %eq.23, pred[]{:T(512)S(6)} %or.3, ...), kind=kLoop, calls=%fused_computation.5 | loop fusion | flops 1179648 | bytes 9437186 | tf_op jit(solution)/shard_map/jit(_where)/select_n | solution.py:89
  235.3 0.9 copy-done.7
  236.2 2.1 fusion.13
  238.3 0.0 reduce-scatter.10.cloned.1.call-update
  238.3 0.0 reduce-scatter.12.cloned.1.call-start
  238.4 3.2 fusion.15
  241.6 0.0 reduce-scatter.12.cloned.1.call-update
  241.6 0.2 reduce-scatter.14.cloned.1.call-start
  241.9 3.3 fusion.17
  245.2 0.0 reduce-scatter.14.cloned.1.call-update
  245.2 0.0 all-gather.2.cloned.1.call-start
  245.3 0.1 reshape.45
  246.1 0.8 dynamic_slice.27
  246.9 0.1 broadcast_subtract_fusion.2
  247.0 0.1 sub.65
  247.1 0.1 sub.61
  247.1 0.1 dynamic_slice.29
  247.2 2.1 multiply_select_fusion
  249.3 0.0 all-gather.2.cloned.1.call-update
  249.3 0.1 fusion.5
  249.4 0.1 fusion.3
  249.5 11.2 %reduce-scatter.10.cloned.1.call-done = f32[48,768]{1,0:T(8,128)} async-done(((f32[192,768]{1,0:T(8,128)}), f32[48,768]{1,0:T(8,128)}) %reduce-scatter.10.cloned.1.call-update) | async-done | bytes 147472 | tf_op jit(solution)/shard_map/reduce_scatter | solution.py:35
  260.7 24.4 %reduce-scatter.12.cloned.1.call-done = f32[48,768]{1,0:T(8,128)} async-done(((f32[192,768]{1,0:T(8,128)}), f32[48,768]{1,0:T(8,128)}) %reduce-scatter.12.cloned.1.call-update) | async-done | bytes 147472 | tf_op jit(solution)/shard_map/reduce_scatter | solution.py:35
  285.2 24.4 %reduce-scatter.14.cloned.1.call-done = f32[48,768]{1,0:T(8,128)} async-done(((f32[192,768]{1,0:T(8,128)}), f32[48,768]{1,0:T(8,128)}) %reduce-scatter.14.cloned.1.call-update) | async-done | bytes 147472 | tf_op jit(solution)/shard_map/reduce_scatter | solution.py:35
  309.6 1.3 multiply_select_fusion.4
  310.9 7.0 %all_gather.16 = f32[192,768]{1,0:T(8,128)S(1)} all-gather(f32[48,768]{1,0:T(8,128)S(1)} %get-tuple-element.18), channel_id=1, replica_groups=mesh['grp'=2,'occ'=4,'aux'=4] {'aux'}, dimensions={0}, use_global_device_ids=true | all-gather | bytes 737280 | tf_op jit(solution)/shard_map/all_gather | solution.py:38
  317.9 11.0 %all_gather.17 = f32[192,768]{1,0:T(8,128)S(1)} all-gather(f32[48,768]{1,0:T(8,128)S(1)} %get-tuple-element.19), channel_id=1, replica_groups=mesh['grp'=2,'occ'=4,'aux'=4] {'aux'}, dimensions={0}, use_global_device_ids=true | all-gather | bytes 737280 | tf_op jit(solution)/shard_map/all_gather | solution.py:38
  328.9 11.4 %all_gather.18 = f32[192,768]{1,0:T(8,128)S(1)} all-gather(f32[48,768]{1,0:T(8,128)S(1)} %get-tuple-element.20), channel_id=1, replica_groups=mesh['grp'=2,'occ'=4,'aux'=4] {'aux'}, dimensions={0}, use_global_device_ids=true | all-gather | bytes 737280 | tf_op jit(solution)/shard_map/all_gather | solution.py:38
  340.3 8.1 %all_gather.19 = f32[192,768]{1,0:T(8,128)} all-gather(f32[48,768]{1,0:T(8,128)S(1)} %get-tuple-element.21), channel_id=1, replica_groups=mesh['grp'=2,'occ'=4,'aux'=4] {'aux'}, dimensions={0}, use_global_device_ids=true | all-gather | bytes 737280 | tf_op jit(solution)/shard_map/all_gather | solution.py:38
  348.4 3.4 fusion.12
  351.7 3.3 fusion.14
  355.1 3.3 fusion.16
  358.4 6.2 %fusion.10 = f32[1024,768]{1,0:T(8,128)S(1)} fusion(f32[1024,768]{0,1:T(8,128)S(1)} %copy-done.2, f32[768,768]{1,0:T(8,128)} %all-gather.2.cloned.1.call-done), kind=kOutput, calls=%fused_computation.36 | convolution fusion | flops 3623878656 | bytes 8650752 | tf_op jit(solution)/shard_map/dot_general | solution.py:42
  364.6 5.7 %add_add_fusion = f32[1024,768]{1,0:T(8,128)} fusion(f32[1024,768]{1,0:T(8,128)} %fusion.16, f32[1024,768]{1,0:T(8,128)S(1)} %copy-done.4, f32[1024,768]{1,0:T(8,128)S(1)} %fusion.10, f32[1024,768]{1,0:T(8,128)S(1)} %copy-done.3, f32[1024,192]{0,1:T(8,128)S(1)} %copy-done.5, f32[192,768]{1,0:T(8,128)S(1)} %copy-done.11), kind=kOutput, calls=%fused_computation | convolution fusion | flops 909115392 | bytes 17104896 | tf_op jit(solution)/shard_map/dot_general | solution.py:42
  (32 shorter events, 0.1 us)
Async XLA Ops:
  6.5 240.7 %reduce-scatter.6.cloned.1.call-start = ((), (), s32[]{:S(2)}) async-start(), calls=%async_computation.5 | async-start | bytes 2949120 | tf_op jit(solution)/shard_map/reduce_scatter | solution.py:35
  10.1 73.4 %collective-permute-start = (f32[1024,768]{0,1:T(8,128)}, f32[1024,768]{0,1:T(8,128)}, u32[]{:S(2)}, u32[]{:S(2)}) collective-permute-start(f32[1024,768]{0,1:T(8,128)} %copy.6), channel_id=1, source_target_pairs={{4,0},{8,4},{12,8},{5,1},{9,5},{13,9},{6,2},{10,6},{14,10},{7,3},{... | collective-permute-start | bytes 9437192 | tf_op jit(solution)/shard_map/ppermute | solution.py:73
  11.4 73.3 %collective-permute-start.1 = (f32[1024,768]{0,1:T(8,128)}, f32[1024,768]{0,1:T(8,128)}, u32[]{:S(2)}, u32[]{:S(2)}) collective-permute-start(f32[1024,768]{0,1:T(8,128)} %copy.6), channel_id=1, source_target_pairs={{0,4},{4,8},{8,12},{1,5},{5,9},{9,13},{2,6},{6,10},{10,14},{3,7},{... | collective-permute-start | bytes 9437192 | tf_op jit(solution)/shard_map/ppermute | solution.py:72
  18.6 73.2 %copy-start = (f32[1024,768]{1,0:T(8,128)S(1)}, f32[1024,768]{1,0:T(8,128)}, u32[]{:S(2)}) copy-start(f32[1024,768]{1,0:T(8,128)} %param.5) | copy-start | bytes 9437188
  90.2 1.6 copy-start.1
  97.2 152.3 %reduce-scatter.8.cloned.1.call-start = ((), (), s32[]{:S(2)}) async-start(), calls=%async_computation.7 | async-start | bytes 737280 | tf_op jit(solution)/shard_map/reduce_scatter | solution.py:35
  100.9 7.0 %collective-permute-start.2 = (f32[1024,192]{0,1:T(8,128)}, f32[1024,192]{0,1:T(8,128)}, u32[]{:S(2)}, u32[]{:S(2)}) collective-permute-start(f32[1024,192]{0,1:T(8,128)} %get-tuple-element.11), channel_id=1, source_target_pairs={{4,8},{8,4},{5,9},{9,5},{6,10},{10,6},{7,11},{11,7},{20,24},{24,20... | collective-permute-start | bytes 2359304 | tf_op jit(solution)/shard_map/ppermute | solution.py:86
  103.1 8.6 %collective-permute-start.4 = (f32[1024,192]{0,1:T(8,128)}, f32[1024,192]{0,1:T(8,128)}, u32[]{:S(2)}, u32[]{:S(2)}) collective-permute-start(f32[1024,192]{0,1:T(8,128)} %get-tuple-element.14), channel_id=1, source_target_pairs={{4,8},{8,4},{5,9},{9,5},{6,10},{10,6},{7,11},{11,7},{20,24},{24,20... | collective-permute-start | bytes 2359304 | tf_op jit(solution)/shard_map/ppermute | solution.py:86
  104.7 7.1 %collective-permute-start.6 = (f32[1024,192]{0,1:T(8,128)}, f32[1024,192]{0,1:T(8,128)}, u32[]{:S(2)}, u32[]{:S(2)}) collective-permute-start(f32[1024,192]{0,1:T(8,128)} %get-tuple-element.13), channel_id=1, source_target_pairs={{4,8},{8,4},{5,9},{9,5},{6,10},{10,6},{7,11},{11,7},{20,24},{24,20... | collective-permute-start | bytes 2359304 | tf_op jit(solution)/shard_map/ppermute | solution.py:86
  106.3 5.5 %collective-permute-start.8 = (f32[1024,192]{0,1:T(8,128)}, f32[1024,192]{0,1:T(8,128)}, u32[]{:S(2)}, u32[]{:S(2)}) collective-permute-start(f32[1024,192]{0,1:T(8,128)} %get-tuple-element.12), channel_id=1, source_target_pairs={{4,8},{8,4},{5,9},{9,5},{6,10},{10,6},{7,11},{11,7},{20,24},{24,20... | collective-permute-start | bytes 2359304 | tf_op jit(solution)/shard_map/ppermute | solution.py:86
  110.5 33.8 %collective-permute-start.3 = (f32[1024,192]{0,1:T(8,128)}, f32[1024,192]{0,1:T(8,128)}, u32[]{:S(2)}, u32[]{:S(2)}) collective-permute-start(f32[1024,192]{0,1:T(8,128)} %slice_select_fusion.3), channel_id=1, source_target_pairs={{8,12},{4,0},{9,13},{5,1},{10,14},{6,2},{11,15},{7,3},{24,28},{20,... | collective-permute-start | bytes 2359304 | tf_op jit(solution)/shard_map/ppermute | solution.py:88
  149.1 3.9 %copy-start.9 = (f32[1024,192]{0,1:T(8,128)}, f32[1024,192]{0,1:T(8,128)S(1)}, u32[]{:S(2)}) copy-start(f32[1024,192]{0,1:T(8,128)S(1)} %get-tuple-element.7) | copy-start | bytes 2359300
  149.1 50.5 %collective-permute-start.5 = (f32[1024,192]{0,1:T(8,128)}, f32[1024,192]{0,1:T(8,128)}, u32[]{:S(2)}, u32[]{:S(2)}) collective-permute-start(f32[1024,192]{0,1:T(8,128)} %get-tuple-element.8), channel_id=1, source_target_pairs={{8,12},{4,0},{9,13},{5,1},{10,14},{6,2},{11,15},{7,3},{24,28},{20,... | collective-permute-start | bytes 2359304 | tf_op jit(solution)/shard_map/ppermute | solution.py:88
  150.4 66.1 %collective-permute-start.7 = (f32[1024,192]{0,1:T(8,128)}, f32[1024,192]{0,1:T(8,128)}, u32[]{:S(2)}, u32[]{:S(2)}) collective-permute-start(f32[1024,192]{0,1:T(8,128)} %get-tuple-element.9), channel_id=1, source_target_pairs={{8,12},{4,0},{9,13},{5,1},{10,14},{6,2},{11,15},{7,3},{24,28},{20,... | collective-permute-start | bytes 2359304 | tf_op jit(solution)/shard_map/ppermute | solution.py:88
  151.7 79.1 %collective-permute-start.9 = (f32[1024,192]{0,1:T(8,128)}, f32[1024,192]{0,1:T(8,128)}, u32[]{:S(2)}, u32[]{:S(2)}) collective-permute-start(f32[1024,192]{0,1:T(8,128)} %get-tuple-element.10), channel_id=1, source_target_pairs={{8,12},{4,0},{9,13},{5,1},{10,14},{6,2},{11,15},{7,3},{24,28},{20,... | collective-permute-start | bytes 2359304 | tf_op jit(solution)/shard_map/ppermute | solution.py:88
  155.1 105.6 %reduce-scatter.10.cloned.1.call-start = ((), (), s32[]{:S(2)}) async-start(), calls=%async_computation.8 | async-start | bytes 737280 | tf_op jit(solution)/shard_map/reduce_scatter | solution.py:35
  235.3 0.9 copy-start.7
  238.3 46.9 %reduce-scatter.12.cloned.1.call-start = ((), (), s32[]{:S(2)}) async-start(), calls=%async_computation.9 | async-start | bytes 737280 | tf_op jit(solution)/shard_map/reduce_scatter | solution.py:35
  241.6 3.7 copy-start.12
  241.6 68.0 %reduce-scatter.14.cloned.1.call-start = ((), (), s32[]{:S(2)}) async-start(), calls=%async_computation.10 | async-start | bytes 737280 | tf_op jit(solution)/shard_map/reduce_scatter | solution.py:35
  245.2 103.2 %copy-start.10 = (f32[1024,192]{0,1:T(8,128)S(1)}, f32[1024,192]{0,1:T(8,128)}, u32[]{:S(2)}) copy-start(f32[1024,192]{0,1:T(8,128)} %copy-done.9) | copy-start | bytes 2359300
  245.2 113.2 %all-gather.2.cloned.1.call-start = ((), (), s32[]{:S(2)}) async-start(), calls=%async_computation.6 | async-start | bytes 2949120 | tf_op jit(solution)/shard_map/all_gather | solution.py:38
  328.9 22.8 %copy-start.8 = (f32[1024,192]{0,1:T(8,128)S(1)}, f32[1024,192]{0,1:T(8,128)}, u32[]{:S(2)}) copy-start(f32[1024,192]{0,1:T(8,128)} %copy-done.7) | copy-start | bytes 2359300
  351.7 3.3 copy-start.6
  355.1 3.3 copy-start.2
  358.4 6.2 %copy-start.3 = (f32[1024,768]{1,0:T(8,128)S(1)}, f32[1024,768]{1,0:T(8,128)}, u32[]{:S(2)}) copy-start(f32[1024,768]{1,0:T(8,128)} %fusion.12) | copy-start | bytes 9437188
  358.4 6.2 %copy-start.4 = (f32[1024,768]{1,0:T(8,128)S(1)}, f32[1024,768]{1,0:T(8,128)}, u32[]{:S(2)}) copy-start(f32[1024,768]{1,0:T(8,128)} %fusion.14) | copy-start | bytes 9437188
  358.4 6.2 %copy-start.5 = (f32[1024,192]{0,1:T(8,128)S(1)}, f32[1024,192]{0,1:T(8,128)}, u32[]{:S(2)}) copy-start(f32[1024,192]{0,1:T(8,128)} %get-tuple-element.16) | copy-start | bytes 2359300
  358.4 6.2 %copy-start.11 = (f32[192,768]{1,0:T(8,128)S(1)}, f32[192,768]{1,0:T(8,128)}, u32[]{:S(2)}) copy-start(f32[192,768]{1,0:T(8,128)} %all_gather.19) | copy-start | bytes 1769476
Sparse Core Ops, SparseCore 0:
  97.4 36.7 reduce-scatter.5
  155.2 53.5 reduce-scatter.7
  238.4 22.2 reduce-scatter.9
  263.1 22.0 reduce-scatter.11
  287.5 22.0 reduce-scatter.13
  311.0 30.3 all-gather.1

commit v2 on v1

--- a/solution.py
+++ b/solution.py
@@ -1,13 +1,19 @@
+import functools
+
 import jax
 import jax.numpy as jnp
 from jax import lax
+from jax.experimental import pallas as pl
+from jax.experimental.pallas import tpu as pltpu
 from jax.sharding import PartitionSpec as P
 
 VT = 192
 BLK = 4
 DMAX = 3
-CHUNKS = 4
+WIDTH = 128
 LINE = 4
+SHARDS = 4
+MESH = pl.DeviceIdType.MESH
 
 PRECISE = lax.Precision.HIGH
 
@@ -61,39 +67,247 @@
     return total
 
 
+def split(x):
+    high = x.astype(jnp.bfloat16)
+    return high, (x - high.astype(jnp.float32)).astype(jnp.bfloat16)
+
+
+def dot3(left, right, dims):
+    dot = functools.partial(lax.dot_general, dimension_numbers=(dims, ((), ())), preferred_element_type=jnp.float32)
+    return dot(left[0], right[0]) + (dot(left[0], right[1]) + dot(left[1], right[0]))
+
+
+def line_kernel(
+    occ, aux, own, odd_ref, own_gaps, gaps, weights, out,
+    near, other, across, relay, own_hi, own_lo, far_hi, far_lo,
+    ints, core_in, half, x_in, amp,
+    near_s, near_r, other_s, other_r, fwd_s, relay_s, across_r,
+    a_s, a_r, b_s, b_r, c_s, c_r,
+):
+    chunks, rows, width = near.shape
+    tile_width = own.shape[1]
+    share = width // 2
+    me = lax.axis_index("occ")
+    rank = lax.axis_index("aux")
+    inner = jnp.logical_and(me > 0, me < occ - 1)
+    side = {"occ": me + 1 - 2 * (me % 2)}
+    middle = {"occ": occ - 1 - me}
+    core = {"aux": rank + 1 - 2 * (rank % 2)}
+    xpeer = {"aux": (rank + 2) % aux}
+    mine = pl.multiple_of((rank % 2) * share, share)
+    theirs = pl.multiple_of((1 - rank % 2) * share, share)
+
+    def remote(src, dst, send, recv, target):
+        return pltpu.make_async_remote_copy(
+            src_ref=src, dst_ref=dst, send_sem=send, recv_sem=recv, device_id=target, device_id_type=MESH
+        )
+
+    def columns(c):
+        return pl.ds(pl.multiple_of(c * width, width), width)
+
+    def near_copy(c):
+        return remote(own.at[:, columns(c)], near.at[c], near_s.at[c], near_r.at[c], side)
+
+    def other_copy(c):
+        return remote(own.at[:, columns(c)], other.at[c], other_s.at[c], other_r.at[c], middle)
+
+    def forward_copy(c):
+        return remote(near.at[c], across.at[c], fwd_s.at[c], across_r.at[c], middle)
+
+    def relay_copy(c):
+        return remote(relay.at[c], across.at[c], relay_s.at[c], across_r.at[c], side)
+
+    def a_copy(i):
+        return remote(ints.at[i, pl.ds(theirs, share)], core_in.at[i], a_s.at[i], a_r.at[i], core)
+
+    def b_copy(i):
+        return remote(half.at[i], x_in.at[i], b_s.at[i], b_r.at[i], xpeer)
+
+    def c_copy(i):
+        rows_of = amp.at[i, pl.ds(mine, share)]
+        return remote(rows_of, rows_of, c_s.at[i], c_r.at[i], core)
+
+    barrier = pltpu.get_barrier_semaphore()
+    for target in (side, core, xpeer):
+        pl.semaphore_signal(barrier, inc=1, device_id=target, device_id_type=MESH)
+
+    @pl.when(inner)
+    def _():
+        pl.semaphore_signal(barrier, inc=1, device_id=middle, device_id_type=MESH)
+        pl.semaphore_wait(barrier, 4)
+
+    @pl.when(jnp.logical_not(inner))
+    def _():
+        pl.semaphore_wait(barrier, 3)
+
+    @pl.loop(0, chunks)
+    def _(c):
+        near_copy(c).start()
+
+        @pl.when(inner)
+        def _():
+            other_copy(c).start()
+
+    band = 256
+
+    @pl.loop(0, rows // band)
+    def _(t):
+        span = pl.ds(pl.multiple_of(t * band, band), band)
+        own_hi[span, :], own_lo[span, :] = split(own[span, :])
+        out[span, :] = jnp.zeros((band, tile_width), jnp.float32)
+
+    def store_far(slot, span, far):
+        far_hi[slot, span, :], far_lo[slot, span, :] = split(far)
+
+    def front(i, slot):
+        c = i % chunks
+
+        @pl.when(i < chunks)
+        def _():
+            near_copy(c).wait_recv()
+
+            @pl.when(inner)
+            def _():
+                forward_copy(c).start()
+
+            @pl.loop(0, rows // band)
+            def _(t):
+                span = pl.ds(pl.multiple_of(t * band, band), band)
+                store_far(slot, span, near[c, span, :])
+
+        @pl.when(i >= chunks)
+        def _():
+            @pl.when(inner)
+            def _():
+                other_copy(c).wait_recv()
+                forward_copy(c).wait_recv()
+                odd = jnp.broadcast_to(odd_ref[...], (band, width)) > 0
+
+                @pl.loop(0, rows // band)
+                def _(t):
+                    span = pl.ds(pl.multiple_of(t * band, band), band)
+                    relay[c, span, :] = jnp.where(odd, across[c, span, :], other[c, span, :])
+
+                relay_copy(c).start()
+
+                @pl.loop(0, rows // band)
+                def _(t):
+                    span = pl.ds(pl.multiple_of(t * band, band), band)
+                    store_far(slot, span, jnp.where(odd, other[c, span, :], across[c, span, :]))
+
+            @pl.when(jnp.logical_not(inner))
+            def _():
+                relay_copy(c).wait_recv()
+
+                @pl.loop(0, rows // band)
+                def _(t):
+                    span = pl.ds(pl.multiple_of(t * band, band), band)
+                    store_far(slot, span, across[c, span, :])
+
+        for n in range(0, tile_width, band):
+            cols = slice(n, n + band)
+            ints[i, :, cols] = dot3(
+                (far_hi[slot], far_lo[slot]), (own_hi[:, cols], own_lo[:, cols]), ((0,), (0,))
+            )
+        a_copy(i).start()
+
+    items = 2 * chunks
+
+    @pl.loop(0, items + 1)
+    def _(i):
+        slot, back = i % 2, (i + 1) % 2
+
+        @pl.when(i < items)
+        def _():
+            front(i, slot)
+
+        @pl.when(i > 0)
+        def _():
+            j = i - 1
+            b_copy(j).wait_recv()
+            at = pl.ds(pl.multiple_of(j * width + mine, share), share)
+            total = half[j] + x_in[j]
+            amp[j, pl.ds(mine, share), :] = weights[at, :] * (total / (gaps[at, :] + own_gaps[...]))
+            c_copy(j).start()
+
+        @pl.when(i < items)
+        def _():
+            a_copy(i).wait_recv()
+            half[i] = ints[i, pl.ds(mine, share), :] + core_in[i]
+            b_copy(i).start()
+
+        @pl.when(i > 0)
+        def _():
+            j = i - 1
+            c_copy(j).wait_recv()
+            amp_parts = split(amp[j])
+
+            @pl.loop(0, rows // band)
+            def _(t):
+                span = pl.ds(pl.multiple_of(t * band, band), band)
+                out[span, :] += dot3((far_hi[back, span, :], far_lo[back, span, :]), amp_parts, ((1,), (0,)))
+
+    @pl.loop(0, chunks)
+    def _(c):
+        near_copy(c).wait_send()
+
+        @pl.when(inner)
+        def _():
+            other_copy(c).wait_send()
+            forward_copy(c).wait_send()
+            relay_copy(c).wait_send()
+
+    @pl.loop(0, items)
+    def _(i):
+        a_copy(i).wait_send()
+        b_copy(i).wait_send()
+        c_copy(i).wait_send()
+
+
 def local_line(factors, eps_occ, eps_vir, tile_index, pair_offset):
     count = lax.axis_size("occ")
+    aux_count = lax.axis_size("aux")
     me = lax.axis_index("occ")
+    rows, tile_width = factors.shape
     vir_energy = lax.dynamic_slice_in_dim(eps_vir, tile_index[0] * VT, VT)
     energy = eps_occ.reshape(count, BLK)
-    own_gaps = gaps_of(vir_energy, energy[me])
     odd = pair_offset[0] % 2 == 1
-    inner = (me == 1) | (me == 2)
-    lower = lax.ppermute(factors, "occ", [(i, i + 1) for i in range(count - 1)])
-    upper = lax.ppermute(factors, "occ", [(i + 1, i) for i in range(count - 1)])
-    near = jnp.where(me % 2 == 0, upper, lower)
-    other = jnp.where(me % 2 == 0, lower, upper)
-    near_block = jnp.where(me % 2 == 0, me + 1, me - 1)
-    near_gaps = gaps_of(vir_energy, energy[near_block])
-    near_amp = amplitude_of(factors, near, own_gaps, near_gaps, jnp.where(odd, 1.0, 0.0))
-    total = term(near, near_amp)
+    near_block = me + 1 - 2 * (me % 2)
     far_block = jnp.where(odd, jnp.where(me % 2 == 0, me - 1, me + 1), me + 2) % count
-    far_gaps = gaps_of(vir_energy, energy[far_block])
-    weight = jnp.where(odd, 1.0, 2.0)
-    width = factors.shape[1] // CHUNKS
-    for chunk in range(CHUNKS):
-        cols = slice(chunk * width, (chunk + 1) * width)
-        across = lax.ppermute(near[:, cols], "occ", [(1, 2), (2, 1)])
-        relay = jnp.where(odd, across, other[:, cols])
-        ends = lax.ppermute(relay, "occ", [(2, 3), (1, 0)])
-        far = jnp.where(inner, jnp.where(odd, other[:, cols], across), ends)
-        amp = amplitude_of(factors, far, own_gaps, far_gaps[cols], weight)
-        total = total + term(far, amp)
-    return total
+    own_gaps = gaps_of(vir_energy, energy[me]).reshape(1, tile_width)
+    blocks = jnp.stack([energy[near_block], energy[far_block]]).reshape(2 * BLK)
+    gaps = gaps_of(vir_energy, blocks).reshape(2 * tile_width, 1)
+    scale = jnp.where(odd, 1.0, jnp.array([0.0, 2.0], jnp.float32))
+    weights = jnp.repeat(scale, tile_width).reshape(2 * tile_width, 1)
+    odd_row = jnp.full((1, WIDTH), odd, jnp.float32)
+    chunks = tile_width // WIDTH
+    items = 2 * chunks
+    f32, half = jnp.float32, jnp.bfloat16
+    block = pltpu.VMEM((chunks, rows, WIDTH), f32)
+    share = pltpu.VMEM((items, WIDTH // 2, tile_width), f32)
+    dma = pltpu.SemaphoreType.DMA
+    vmem = pl.BlockSpec(memory_space=pltpu.VMEM)
+    return pl.pallas_call(
+        functools.partial(line_kernel, count, aux_count),
+        out_shape=jax.ShapeDtypeStruct((rows, tile_width), f32),
+        in_specs=[vmem] * 5,
+        out_specs=vmem,
+        scratch_shapes=[block] * 4
+        + [pltpu.VMEM((rows, tile_width), half)] * 2
+        + [pltpu.VMEM((2, rows, WIDTH), half)] * 2
+        + [pltpu.VMEM((items, WIDTH, tile_width), f32), share, share, share]
+        + [pltpu.VMEM((items, WIDTH, tile_width), f32)]
+        + [dma((chunks,))] * 7
+        + [dma((items,))] * 6,
+        compiler_params=pltpu.CompilerParams(
+            collective_id=0, has_side_effects=True, vmem_limit_bytes=56 * 1024 * 1024
+        ),
+        name="pair_line",
+    )(factors, odd_row, own_gaps, gaps, weights)
 
 
 def solution(mesh):
     in_specs = (P(("grp", "aux"), "occ"), P("grp"), P("grp"), P("grp"), P("grp"))
     out_specs = P(("grp", "aux"), "occ")
-    body = local_line if mesh.shape["occ"] == LINE else local_ring
+    body = local_line if mesh.shape["occ"] == LINE and mesh.shape["aux"] == SHARDS else local_ring
     return jax.shard_map(body, mesh=mesh, in_specs=in_specs, out_specs=out_specs, check_vma=False)

time: 378 us -> 180 us (0.48)
  waiting for transfers between devices: 234 us -> 0 us
  Pallas kernels: 0 us -> 169 us
  matrix products: 38 us -> 0 us
  blocking collectives: 37.4 us -> 0 us
  other arithmetic: 20.9 us -> 0.16 us
  starting transfers between devices: 20.3 us -> 0 us
  between operations: 15.1 us -> 1.36 us
    ppermute x10 -> x0, waiting for transfers between devices: 174 us -> none  [the longest x4 108 us: local_line(): ends = lax.ppermute(relay, 'occ', [(2, 3), (1, 0)])]
    pallas_call x0 -> x1, Pallas kernels: none -> 169 us  [local_line(): pl.pallas_call(functools.partial(line_kernel, count, aux_count), out_shap...]
    reduce_scatter x5 -> x0, waiting for transfers between devices: 60.1 us -> none  [amplitude_of(): lax.psum_scatter(inner_dot(far, own), 'aux', scatter_dimension=0, tiled=T...]
    dot_general x10 -> x0, matrix products: 38 us -> none  [the longest x5 21.8 us: term(): jnp.dot(far, amplitude, precision=PRECISE, preferred_element_type=jnp.flo...]
    all_gather x4 -> x0, blocking collectives: 37.4 us -> none  [amplitude_of(): return lax.all_gather(amplitude, 'aux', axis=0, tiled=True)]
    select_n x6 -> x1, other arithmetic: 20.8 us -> 0.01 us  [local_line(): scale = jnp.where(odd, 1.0, jnp.array([0.0, 2.0], jnp.float32))]
    ppermute x10 -> x0, starting transfers between devices: 19.9 us -> none  [the longest x1 7.23 us: local_line(): lower = lax.ppermute(factors, 'occ', [(i, i + 1) for i in range(count - 1)])]
  transfers between devices with their start and end apart: 16 -> 0, of which waited for: 9 -> 0; matrix products, arithmetic and copies ran while one was open for 11% -> 0% of each run, Pallas kernels for 0% -> 0%
where the time goes in v2:
time: 180 us
  Pallas kernels  169 us (94%)
  local copies, waits for them, and re-layouts  9.32 us (5%)
    pallas_call x1, Pallas kernels, local_line(): pl.pallas_call(functools.partial(line_kernel, count, aux_count), out_shap...  169 us
    unnamed x4, local copies, waits for them, and re-layouts  5.02 us

profile of v2, /device:TPU:0, one launch (start us, length us, event | category | flops | bytes accessed | tf_op | source)
XLA Modules:
  0.0 179.6 jit_solution(15592939692756109842)
XLA Ops:
  1.3 0.5 broadcast_in_dim.12.odd_ref
  1.9 0.8 dynamic_slice.12
  2.7 0.7 reshape.52
  3.4 0.1 sub.64
  3.5 0.1 broadcast_subtract_fusion.1
  3.6 0.7 sub.60.own_gaps
  4.2 0.1 broadcast_bitcast_fusion
  4.3 0.1 broadcast_subtract_fusion
  4.4 1.5 sub.68.gaps
  5.9 1.2 copy.10
  7.1 168.7 %pair_line.1 = f32[1024,768]{1,0:T(8,128)} custom-call(f32[1024,768]{1,0:T(8,128)} %own.1, f32[1,128]{1,0:T(1,128)} %broadcast_in_dim.12.odd_ref, f32[1,768]{1,0:T(1,128)} %sub.60.own_gaps, f32[1536,1]{1,0:T(8,128)} %sub.68.gaps, f32[1536,1]{1,0:T(8,128)} %bitcast.12), custom_call_target="tpu_custom_call" | custom-call | tf_op jit(solution)/shard_map/pair_line/pallas_call | solution.py:290
  175.8 3.8 %copy.14 = f32[1024,768]{1,0:T(8,128)} copy(f32[1024,768]{1,0:T(8,128)} %pair_line.1) | data formatting | bytes 6291456
  (4 shorter events, 0.0 us)

commit v3 on v2

--- a/solution.py
+++ b/solution.py
@@ -11,6 +11,8 @@
 BLK = 4
 DMAX = 3
 WIDTH = 128
+PARTS = 4
+NTILE = 256
 LINE = 4
 SHARDS = 4
 MESH = pl.DeviceIdType.MESH
@@ -78,15 +80,16 @@
 
 
 def line_kernel(
-    occ, aux, own, odd_ref, own_gaps, gaps, weights, out,
+    occ, aux, own, offset, table, out,
     near, other, across, relay, own_hi, own_lo, far_hi, far_lo,
-    ints, core_in, half, x_in, amp,
+    ints, core_in, half, x_in, amp, own_row, gap_cols,
     near_s, near_r, other_s, other_r, fwd_s, relay_s, across_r,
     a_s, a_r, b_s, b_r, c_s, c_r,
 ):
     chunks, rows, width = near.shape
     tile_width = own.shape[1]
     share = width // 2
+    band = rows // PARTS
     me = lax.axis_index("occ")
     rank = lax.axis_index("aux")
     inner = jnp.logical_and(me > 0, me < occ - 1)
@@ -111,11 +114,16 @@
     def other_copy(c):
         return remote(own.at[:, columns(c)], other.at[c], other_s.at[c], other_r.at[c], middle)
 
-    def forward_copy(c):
-        return remote(near.at[c], across.at[c], fwd_s.at[c], across_r.at[c], middle)
-
-    def relay_copy(c):
-        return remote(relay.at[c], across.at[c], relay_s.at[c], across_r.at[c], side)
+    def band_of(t):
+        return pl.ds(pl.multiple_of(t * band, band), band)
+
+    def forward_copy(c, t):
+        span = band_of(t)
+        return remote(near.at[c, span], across.at[c, span], fwd_s.at[c, t], across_r.at[c, t], middle)
+
+    def relay_copy(c, t):
+        span = band_of(t)
+        return remote(relay.at[c, span], across.at[c, span], relay_s.at[c, t], across_r.at[c, t], side)
 
     def a_copy(i):
         return remote(ints.at[i, pl.ds(theirs, share)], core_in.at[i], a_s.at[i], a_r.at[i], core)
@@ -148,19 +156,51 @@
         def _():
             other_copy(c).start()
 
-    band = 256
-
-    @pl.loop(0, rows // band)
+    items = 2 * chunks
+    odd = offset[0] & 1
+
+    @pl.loop(0, PARTS)
     def _(t):
-        span = pl.ds(pl.multiple_of(t * band, band), band)
+        span = band_of(t)
         own_hi[span, :], own_lo[span, :] = split(own[span, :])
         out[span, :] = jnp.zeros((band, tile_width), jnp.float32)
 
-    def store_far(slot, span, far):
-        far_hi[slot, span, :], far_lo[slot, span, :] = split(far)
+    for r in range(chunks):
+        own_row[:, r * width : (r + 1) * width] = table[r : r + 1, :]
+
+    @pl.loop(0, items)
+    def _(i):
+        gap_cols[i] = jnp.broadcast_to(table[pl.ds(chunks + i, 1), :], (width, width)).T
+
+    def pick(odd_one, even_one):
+        return jnp.where(jnp.full((band, width), odd, jnp.int32) > 0, odd_one, even_one)
+
+    def serve(c, t):
+        @pl.when(inner)
+        def _():
+            if t == 0:
+                other_copy(c).wait_recv()
+            forward_copy(c, t).wait_recv()
+            span = band_of(t)
+            relay[c, span, :] = pick(across[c, span, :], other[c, span, :])
+            relay_copy(c, t).start()
+
+    def serve_next(i, t):
+        @pl.when(jnp.logical_and(i >= chunks - 1, i < items - 1))
+        def _():
+            serve(i + 1 - chunks, t)
+
+    def integrals(i, slot, t, far):
+        span = band_of(t)
+        parts = split(far)
+        far_hi[slot, span, :], far_lo[slot, span, :] = parts
+        for n in range(0, tile_width, NTILE):
+            cols = slice(n, n + NTILE)
+            ints[i, :, cols] += dot3(parts, (own_hi[span, cols], own_lo[span, cols]), ((0,), (0,)))
 
     def front(i, slot):
         c = i % chunks
+        ints[i] = jnp.zeros((width, tile_width), jnp.float32)
 
         @pl.when(i < chunks)
         def _():
@@ -168,50 +208,33 @@
 
             @pl.when(inner)
             def _():
-                forward_copy(c).start()
-
-            @pl.loop(0, rows // band)
+                @pl.loop(0, PARTS)
+                def _(t):
+                    forward_copy(c, t).start()
+
+            @pl.loop(0, PARTS)
             def _(t):
-                span = pl.ds(pl.multiple_of(t * band, band), band)
-                store_far(slot, span, near[c, span, :])
+                integrals(i, slot, t, near[c, band_of(t), :])
 
         @pl.when(i >= chunks)
         def _():
+            serve(c, PARTS - 1)
+
             @pl.when(inner)
             def _():
-                other_copy(c).wait_recv()
-                forward_copy(c).wait_recv()
-                odd = jnp.broadcast_to(odd_ref[...], (band, width)) > 0
-
-                @pl.loop(0, rows // band)
+                @pl.loop(0, PARTS)
                 def _(t):
-                    span = pl.ds(pl.multiple_of(t * band, band), band)
-                    relay[c, span, :] = jnp.where(odd, across[c, span, :], other[c, span, :])
-
-                relay_copy(c).start()
-
-                @pl.loop(0, rows // band)
-                def _(t):
-                    span = pl.ds(pl.multiple_of(t * band, band), band)
-                    store_far(slot, span, jnp.where(odd, other[c, span, :], across[c, span, :]))
+                    span = band_of(t)
+                    integrals(i, slot, t, pick(other[c, span, :], across[c, span, :]))
 
             @pl.when(jnp.logical_not(inner))
             def _():
-                relay_copy(c).wait_recv()
-
-                @pl.loop(0, rows // band)
+                @pl.loop(0, PARTS)
                 def _(t):
-                    span = pl.ds(pl.multiple_of(t * band, band), band)
-                    store_far(slot, span, across[c, span, :])
-
-        for n in range(0, tile_width, band):
-            cols = slice(n, n + band)
-            ints[i, :, cols] = dot3(
-                (far_hi[slot], far_lo[slot]), (own_hi[:, cols], own_lo[:, cols]), ((0,), (0,))
-            )
+                    relay_copy(c, t).wait_recv()
+                    integrals(i, slot, t, across[c, band_of(t), :])
+
         a_copy(i).start()
-
-    items = 2 * chunks
 
     @pl.loop(0, items + 1)
     def _(i):
@@ -221,13 +244,19 @@
         def _():
             front(i, slot)
 
+        serve_next(i, 0)
+
         @pl.when(i > 0)
         def _():
             j = i - 1
             b_copy(j).wait_recv()
-            at = pl.ds(pl.multiple_of(j * width + mine, share), share)
-            total = half[j] + x_in[j]
-            amp[j, pl.ds(mine, share), :] = weights[at, :] * (total / (gaps[at, :] + own_gaps[...]))
+            at = pl.ds(mine, share)
+            single = jnp.full((share, width), odd, jnp.int32).astype(jnp.float32)
+            weight = jnp.where(j < chunks, single, 2.0 - single)
+            for r in range(chunks):
+                cols = slice(r * width, (r + 1) * width)
+                total = half[j, :, cols] + x_in[j, :, cols]
+                amp[j, at, cols] = weight * (total / (gap_cols[j, at, :] + own_row[:, cols]))
             c_copy(j).start()
 
         @pl.when(i < items)
@@ -236,16 +265,26 @@
             half[i] = ints[i, pl.ds(mine, share), :] + core_in[i]
             b_copy(i).start()
 
+        serve_next(i, 1)
+
         @pl.when(i > 0)
         def _():
             j = i - 1
             c_copy(j).wait_recv()
-            amp_parts = split(amp[j])
-
-            @pl.loop(0, rows // band)
-            def _(t):
-                span = pl.ds(pl.multiple_of(t * band, band), band)
-                out[span, :] += dot3((far_hi[back, span, :], far_lo[back, span, :]), amp_parts, ((1,), (0,)))
+
+        def add_terms(first, last):
+            @pl.when(i > 0)
+            def _():
+                amp_parts = split(amp[i - 1])
+
+                @pl.loop(first, last)
+                def _(t):
+                    span = band_of(t)
+                    out[span, :] += dot3((far_hi[back, span, :], far_lo[back, span, :]), amp_parts, ((1,), (0,)))
+
+        add_terms(0, PARTS // 2)
+        serve_next(i, 2)
+        add_terms(PARTS // 2, PARTS)
 
     @pl.loop(0, chunks)
     def _(c):
@@ -254,8 +293,11 @@
         @pl.when(inner)
         def _():
             other_copy(c).wait_send()
-            forward_copy(c).wait_send()
-            relay_copy(c).wait_send()
+
+            @pl.loop(0, PARTS)
+            def _(t):
+                forward_copy(c, t).wait_send()
+                relay_copy(c, t).wait_send()
 
     @pl.loop(0, items)
     def _(i):
@@ -274,12 +316,8 @@
     odd = pair_offset[0] % 2 == 1
     near_block = me + 1 - 2 * (me % 2)
     far_block = jnp.where(odd, jnp.where(me % 2 == 0, me - 1, me + 1), me + 2) % count
-    own_gaps = gaps_of(vir_energy, energy[me]).reshape(1, tile_width)
-    blocks = jnp.stack([energy[near_block], energy[far_block]]).reshape(2 * BLK)
-    gaps = gaps_of(vir_energy, blocks).reshape(2 * tile_width, 1)
-    scale = jnp.where(odd, 1.0, jnp.array([0.0, 2.0], jnp.float32))
-    weights = jnp.repeat(scale, tile_width).reshape(2 * tile_width, 1)
-    odd_row = jnp.full((1, WIDTH), odd, jnp.float32)
+    blocks = jnp.stack([energy[me], energy[near_block], energy[far_block]]).reshape(3 * BLK)
+    table = gaps_of(vir_energy, blocks).reshape(3 * tile_width // WIDTH, WIDTH)
     chunks = tile_width // WIDTH
     items = 2 * chunks
     f32, half = jnp.float32, jnp.bfloat16
@@ -290,20 +328,22 @@
     return pl.pallas_call(
         functools.partial(line_kernel, count, aux_count),
         out_shape=jax.ShapeDtypeStruct((rows, tile_width), f32),
-        in_specs=[vmem] * 5,
+        in_specs=[vmem, pl.BlockSpec(memory_space=pltpu.SMEM), vmem],
         out_specs=vmem,
         scratch_shapes=[block] * 4
         + [pltpu.VMEM((rows, tile_width), half)] * 2
         + [pltpu.VMEM((2, rows, WIDTH), half)] * 2
         + [pltpu.VMEM((items, WIDTH, tile_width), f32), share, share, share]
         + [pltpu.VMEM((items, WIDTH, tile_width), f32)]
-        + [dma((chunks,))] * 7
+        + [pltpu.VMEM((1, tile_width), f32), pltpu.VMEM((items, WIDTH, WIDTH), f32)]
+        + [dma((chunks,))] * 4
+        + [dma((chunks, PARTS))] * 3
         + [dma((items,))] * 6,
         compiler_params=pltpu.CompilerParams(
             collective_id=0, has_side_effects=True, vmem_limit_bytes=56 * 1024 * 1024
         ),
         name="pair_line",
-    )(factors, odd_row, own_gaps, gaps, weights)
+    )(factors, pair_offset, table)
 
 
 def solution(mesh):

time: 180 us -> 169 us (0.939)
  Pallas kernels: 169 us -> 161 us
  local copies, waits for them, and re-layouts: 9.32 us -> 6.03 us
    pallas_call x1, Pallas kernels: 169 us -> 161 us  [local_line(): pl.pallas_call(functools.partial(line_kernel, count, aux_count), out_shap...]
    unnamed x4 -> x1, local copies, waits for them, and re-layouts: 5.02 us -> 3.76 us
where the time goes in v3:
time: 169 us
  Pallas kernels  161 us (95%)
  local copies, waits for them, and re-layouts  6.03 us (4%)
    pallas_call x1, Pallas kernels, local_line(): pl.pallas_call(functools.partial(line_kernel, count, aux_count), out_shap...  161 us
    unnamed x1, local copies, waits for them, and re-layouts  3.76 us

profile of v3, /device:TPU:0, one launch (start us, length us, event | category | flops | bytes accessed | tf_op | source)
XLA Modules:
  0.0 168.6 jit_solution(3443039138130648534)
XLA Ops:
  1.3 0.8 dynamic_slice.12
  2.1 0.7 reshape.10
  2.9 0.1 sub.28
  3.0 0.1 broadcast_subtract_fusion
  3.0 0.7 sub.31.table
  3.7 161.1 %pair_line.1 = f32[1024,768]{1,0:T(8,128)} custom-call(f32[1024,768]{1,0:T(8,128)} %own.1, s32[1]{0:T(128)} %copy.8.offset, f32[18,128]{1,0:T(8,128)} %sub.31.table), custom_call_target="tpu_custom_call" | custom-call | tf_op jit(solution)/shard_map/pair_line/pallas_call | solution.py:328
  164.8 3.8 %copy.9 = f32[1024,768]{1,0:T(8,128)} copy(f32[1024,768]{1,0:T(8,128)} %pair_line.1) | data formatting | bytes 6291456
  (2 shorter events, 0.0 us)

commit v4 on v3

--- a/solution.py
+++ b/solution.py
@@ -12,6 +12,7 @@
 DMAX = 3
 WIDTH = 128
 PARTS = 4
+SLOTS = 3
 NTILE = 256
 LINE = 4
 SHARDS = 4
@@ -80,11 +81,11 @@
 
 
 def line_kernel(
-    occ, aux, own, offset, table, out,
+    occ, aux, own, offset, table, total_out, far_out, amp_out, out,
     near, other, across, relay, own_hi, own_lo, far_hi, far_lo,
     ints, core_in, half, x_in, amp, own_row, gap_cols,
     near_s, near_r, other_s, other_r, fwd_s, relay_s, across_r,
-    a_s, a_r, b_s, b_r, c_s, c_r,
+    a_s, a_r, b_s, b_r, c_s, c_r, out_s,
 ):
     chunks, rows, width = near.shape
     tile_width = own.shape[1]
@@ -175,6 +176,19 @@
     def pick(odd_one, even_one):
         return jnp.where(jnp.full((band, width), odd, jnp.int32) > 0, odd_one, even_one)
 
+    def integrals(i, slot, t, far):
+        span = band_of(t)
+        parts = split(far)
+        far_hi[slot, span, :], far_lo[slot, span, :] = parts
+
+        @pl.when(i == items - 1)
+        def _():
+            far_out[span, :] = far
+
+        for n in range(0, tile_width, NTILE):
+            cols = slice(n, n + NTILE)
+            ints[i, :, cols] += dot3(parts, (own_hi[span, cols], own_lo[span, cols]), ((0,), (0,)))
+
     def serve(c, t):
         @pl.when(inner)
         def _():
@@ -184,26 +198,22 @@
             span = band_of(t)
             relay[c, span, :] = pick(across[c, span, :], other[c, span, :])
             relay_copy(c, t).start()
+            i = c + chunks
+            if t == 0:
+                ints[i] = jnp.zeros((width, tile_width), jnp.float32)
+            integrals(i, i % SLOTS, t, pick(other[c, span, :], across[c, span, :]))
 
     def serve_next(i, t):
         @pl.when(jnp.logical_and(i >= chunks - 1, i < items - 1))
         def _():
             serve(i + 1 - chunks, t)
 
-    def integrals(i, slot, t, far):
-        span = band_of(t)
-        parts = split(far)
-        far_hi[slot, span, :], far_lo[slot, span, :] = parts
-        for n in range(0, tile_width, NTILE):
-            cols = slice(n, n + NTILE)
-            ints[i, :, cols] += dot3(parts, (own_hi[span, cols], own_lo[span, cols]), ((0,), (0,)))
-
     def front(i, slot):
         c = i % chunks
-        ints[i] = jnp.zeros((width, tile_width), jnp.float32)
 
         @pl.when(i < chunks)
         def _():
+            ints[i] = jnp.zeros((width, tile_width), jnp.float32)
             near_copy(c).wait_recv()
 
             @pl.when(inner)
@@ -220,15 +230,10 @@
         def _():
             serve(c, PARTS - 1)
 
-            @pl.when(inner)
-            def _():
-                @pl.loop(0, PARTS)
-                def _(t):
-                    span = band_of(t)
-                    integrals(i, slot, t, pick(other[c, span, :], across[c, span, :]))
-
             @pl.when(jnp.logical_not(inner))
             def _():
+                ints[i] = jnp.zeros((width, tile_width), jnp.float32)
+
                 @pl.loop(0, PARTS)
                 def _(t):
                     relay_copy(c, t).wait_recv()
@@ -238,7 +243,11 @@
 
     @pl.loop(0, items + 1)
     def _(i):
-        slot, back = i % 2, (i + 1) % 2
+        slot, back = i % SLOTS, (i + SLOTS - 1) % SLOTS
+
+        @pl.when(i == items)
+        def _():
+            pltpu.make_async_copy(out, total_out, out_s).start()
 
         @pl.when(i < items)
         def _():
@@ -273,7 +282,7 @@
             c_copy(j).wait_recv()
 
         def add_terms(first, last):
-            @pl.when(i > 0)
+            @pl.when(jnp.logical_and(i > 0, i < items))
             def _():
                 amp_parts = split(amp[i - 1])
 
@@ -285,6 +294,9 @@
         add_terms(0, PARTS // 2)
         serve_next(i, 2)
         add_terms(PARTS // 2, PARTS)
+
+    amp_out[...] = amp[items - 1]
+    pltpu.make_async_copy(out, total_out, out_s).wait()
 
     @pl.loop(0, chunks)
     def _(c):
@@ -325,25 +337,32 @@
     share = pltpu.VMEM((items, WIDTH // 2, tile_width), f32)
     dma = pltpu.SemaphoreType.DMA
     vmem = pl.BlockSpec(memory_space=pltpu.VMEM)
-    return pl.pallas_call(
+    total, far, amplitude = pl.pallas_call(
         functools.partial(line_kernel, count, aux_count),
-        out_shape=jax.ShapeDtypeStruct((rows, tile_width), f32),
+        out_shape=[
+            jax.ShapeDtypeStruct((rows, tile_width), f32),
+            jax.ShapeDtypeStruct((rows, WIDTH), f32),
+            jax.ShapeDtypeStruct((WIDTH, tile_width), f32),
+        ],
         in_specs=[vmem, pl.BlockSpec(memory_space=pltpu.SMEM), vmem],
-        out_specs=vmem,
-        scratch_shapes=[block] * 4
+        out_specs=[pl.BlockSpec(memory_space=pl.ANY), vmem, vmem],
+        scratch_shapes=[pltpu.VMEM((rows, tile_width), f32)]
+        + [block] * 4
         + [pltpu.VMEM((rows, tile_width), half)] * 2
-        + [pltpu.VMEM((2, rows, WIDTH), half)] * 2
+        + [pltpu.VMEM((SLOTS, rows, WIDTH), half)] * 2
         + [pltpu.VMEM((items, WIDTH, tile_width), f32), share, share, share]
         + [pltpu.VMEM((items, WIDTH, tile_width), f32)]
         + [pltpu.VMEM((1, tile_width), f32), pltpu.VMEM((items, WIDTH, WIDTH), f32)]
         + [dma((chunks,))] * 4
         + [dma((chunks, PARTS))] * 3
-        + [dma((items,))] * 6,
+        + [dma((items,))] * 6
+        + [dma],
         compiler_params=pltpu.CompilerParams(
             collective_id=0, has_side_effects=True, vmem_limit_bytes=56 * 1024 * 1024
         ),
         name="pair_line",
     )(factors, pair_offset, table)
+    return total + term(far, amplitude)
 
 
 def solution(mesh):

time: 169 us -> 168 us (level)
  matrix products: 0 us -> 5.22 us
  local copies, waits for them, and re-layouts: 6.03 us -> 2.29 us
  Pallas kernels: 161 us -> 159 us
    dot_general x0 -> x1, matrix products: none -> 5.22 us  [term(): jnp.dot(far, amplitude, precision=PRECISE, preferred_element_type=jnp.flo...]
    unnamed x1 -> x0, local copies, waits for them, and re-layouts: 3.76 us -> none
    pallas_call x1, Pallas kernels: 161 us -> 159 us  [local_line(): pl.pallas_call(functools.partial(line_kernel, count, aux_count), out_shap...]
where the time goes in v4:
time: 168 us; the launch traced here: 167 us
  Pallas kernels  159 us (95%)
  matrix products  5.22 us (3%)
  local copies, waits for them, and re-layouts  2.29 us (1%)
    pallas_call x1, Pallas kernels, local_line(): pl.pallas_call(functools.partial(line_kernel, count, aux_count), out_shap...  159 us
    dot_general x1, matrix products, term(): jnp.dot(far, amplitude, precision=PRECISE, preferred_element_type=jnp.flo...  5.22 us

profile of v4, /device:TPU:0, one launch (start us, length us, event | category | flops | bytes accessed | tf_op | source)
XLA Modules:
  0.0 167.5 jit_solution(13274769444185446268)
XLA Ops:
  1.3 0.8 dynamic_slice.12
  2.1 0.7 reshape.10
  2.9 0.1 sub.28
  3.0 0.1 broadcast_subtract_fusion
  3.0 0.7 sub.31.table
  3.7 158.5 %pair_line.1 = (f32[1024,768]{1,0:T(8,128)}, f32[1024,128]{1,0:T(8,128)}, f32[128,768]{1,0:T(8,128)}) custom-call(f32[1024,768]{1,0:T(8,128)} %own.1, s32[1]{0:T(128)} %copy.7.offset, f32[18,128]{1,0:T(8,128)} %sub.31.table), custom_call_target="tpu_custom_call" | custom-call | tf_op jit(solution)/shard_map/pair_line/pallas_call | solution.py:340
  162.2 5.2 %convolution_add_fusion = f32[1024,768]{1,0:T(8,128)} fusion(f32[1024,768]{1,0:T(8,128)} %get-tuple-element.8, f32[1024,128]{1,0:T(8,128)} %get-tuple-element.9, f32[128,768]{1,0:T(8,128)} %get-tuple-element.10), kind=kOutput, calls=%fused_computation | convolution fusion | flops 604766208 | bytes 7208960 | tf_op jit(solution)/shard_map/dot_general | solution.py:51
  (2 shorter events, 0.0 us)

commit v5 on v4

--- a/solution.py
+++ b/solution.py
@@ -13,6 +13,7 @@
 WIDTH = 128
 PARTS = 4
 SLOTS = 3
+AHEAD = 2
 NTILE = 256
 LINE = 4
 SHARDS = 4
@@ -153,7 +154,7 @@
     def _(c):
         near_copy(c).start()
 
-        @pl.when(inner)
+        @pl.when(jnp.logical_and(inner, c < AHEAD))
         def _():
             other_copy(c).start()
 
@@ -221,6 +222,10 @@
                 @pl.loop(0, PARTS)
                 def _(t):
                     forward_copy(c, t).start()
+
+                @pl.when(c + AHEAD < chunks)
+                def _():
+                    other_copy(c + AHEAD).start()
 
             @pl.loop(0, PARTS)
             def _(t):

time: 168 us -> 168 us (level)
  no operation moved by 1% of the time
where the time goes in v5:
time: 168 us; the launch traced here: 167 us
  Pallas kernels  159 us (95%)
  matrix products  5.22 us (3%)
  local copies, waits for them, and re-layouts  2.29 us (1%)
    pallas_call x1, Pallas kernels, local_line(): pl.pallas_call(functools.partial(line_kernel, count, aux_count), out_shap...  159 us
    dot_general x1, matrix products, term(): jnp.dot(far, amplitude, precision=PRECISE, preferred_element_type=jnp.flo...  5.22 us

profile of v5, /device:TPU:0, one launch (start us, length us, event | category | flops | bytes accessed | tf_op | source)
XLA Modules:
  0.0 167.5 jit_solution(5950878847206703783)
XLA Ops:
  1.3 0.8 dynamic_slice.12
  2.1 0.7 reshape.10
  2.9 0.1 sub.28
  3.0 0.1 broadcast_subtract_fusion
  3.0 0.7 sub.31.table
  3.7 158.5 %pair_line.1 = (f32[1024,768]{1,0:T(8,128)}, f32[1024,128]{1,0:T(8,128)}, f32[128,768]{1,0:T(8,128)}) custom-call(f32[1024,768]{1,0:T(8,128)} %own.1, s32[1]{0:T(128)} %copy.7.offset, f32[18,128]{1,0:T(8,128)} %sub.31.table), custom_call_target="tpu_custom_call" | custom-call | tf_op jit(solution)/shard_map/pair_line/pallas_call | solution.py:345
  162.2 5.2 %convolution_add_fusion = f32[1024,768]{1,0:T(8,128)} fusion(f32[1024,768]{1,0:T(8,128)} %get-tuple-element.8, f32[1024,128]{1,0:T(8,128)} %get-tuple-element.9, f32[128,768]{1,0:T(8,128)} %get-tuple-element.10), kind=kOutput, calls=%fused_computation | convolution fusion | flops 604766208 | bytes 7208960 | tf_op jit(solution)/shard_map/dot_general | solution.py:52
  (2 shorter events, 0.0 us)

commit v6 on v4

--- a/solution.py
+++ b/solution.py
@@ -13,7 +13,7 @@
 WIDTH = 128
 PARTS = 4
 SLOTS = 3
-NTILE = 256
+NTILE = 768
 LINE = 4
 SHARDS = 4
 MESH = pl.DeviceIdType.MESH

time: 168 us -> 168 us (level)
  no operation moved by 1% of the time
where the time goes in v6:
time: 168 us; the launch traced here: 167 us
  Pallas kernels  158 us (94%)
  matrix products  5.22 us (3%)
  local copies, waits for them, and re-layouts  2.28 us (1%)
    pallas_call x1, Pallas kernels, local_line(): pl.pallas_call(functools.partial(line_kernel, count, aux_count), out_shap...  158 us
    dot_general x1, matrix products, term(): jnp.dot(far, amplitude, precision=PRECISE, preferred_element_type=jnp.flo...  5.22 us

profile of v6, /device:TPU:0, one launch (start us, length us, event | category | flops | bytes accessed | tf_op | source)
XLA Modules:
  0.0 167.4 jit_solution(3538261297272323147)
XLA Ops:
  1.3 0.8 dynamic_slice.12
  2.1 0.7 reshape.10
  2.9 0.1 sub.28
  3.0 0.1 broadcast_subtract_fusion
  3.0 0.7 sub.31.table
  3.7 158.5 %pair_line.1 = (f32[1024,768]{1,0:T(8,128)}, f32[1024,128]{1,0:T(8,128)}, f32[128,768]{1,0:T(8,128)}) custom-call(f32[1024,768]{1,0:T(8,128)} %own.1, s32[1]{0:T(128)} %copy.7.offset, f32[18,128]{1,0:T(8,128)} %sub.31.table), custom_call_target="tpu_custom_call" | custom-call | tf_op jit(solution)/shard_map/pair_line/pallas_call | solution.py:340
  162.2 5.2 %convolution_add_fusion = f32[1024,768]{1,0:T(8,128)} fusion(f32[1024,768]{1,0:T(8,128)} %get-tuple-element.8, f32[1024,128]{1,0:T(8,128)} %get-tuple-element.9, f32[128,768]{1,0:T(8,128)} %get-tuple-element.10), kind=kOutput, calls=%fused_computation | convolution fusion | flops 604766208 | bytes 7208960 | tf_op jit(solution)/shard_map/dot_general | solution.py:51
  (2 shorter events, 0.0 us)
